TPU v7x, 32 devices: a whole 2x2x4 slice. The times are simulated.
32 devices in a mesh: wide: 8 (over z, x), narrow: 4 (over y, core).
Axes of the slice: x: 2, y: 2, z: 4, core: 2. Of those that a mesh axis runs over, the one named last changes fastest.
Arguments:
- embeddings: bfloat16 [16384, 1024], P(('wide', 'narrow')), may hold values from -32 to 32
- valid: int32 [16384], P(('wide', 'narrow')), may hold values from 0 to 1, as said below
Outputs:
- whitened: bfloat16 [16384, 1024], P(('wide', 'narrow'))
Inputs may be any that keep to these rules, and one draw needn't show every extreme that they name: The first row of every aligned block of 16 rows has valid = 1.
All inputs are finite; a program needn't handle non-finite values.
Results may differ from a plain program's by a relative error of at most 0.001.
Values sent between devices are 32-bit elements; how exact they have to be, the bound alone decides.
No kernel may reach another device: no remote copies, remote signals or barrier semaphores. Data moves between devices by JAX's collectives and lax.ppermute only.
A program may use at most 64 MiB of HBM per device.

v0:
```python
import jax
import jax.numpy as jnp
from jax import lax
from jax.sharding import PartitionSpec as P


def shifted_scatter(gram, count_local, sums_local, center):
    return (
        gram
        - sums_local[:, None] * center[None, :]
        - center[:, None] * sums_local[None, :]
        + count_local * center[:, None] * center[None, :]
    )


def narrow_rows(term):
    return lax.psum_scatter(term, "narrow", scatter_dimension=0, tiled=True)


def on_device(embeddings, valid):
    width = embeddings.shape[1]
    narrow_count = lax.axis_size("narrow")
    row_span = width // narrow_count
    offset = lax.axis_index("narrow") * row_span
    mask_half = valid.astype(jnp.bfloat16)
    count_local = jnp.sum(valid.astype(jnp.float32))
    masked = embeddings * mask_half[:, None]
    gram = lax.dot_general(
        masked, embeddings, (((0,), (0,)), ((), ())), preferred_element_type=jnp.float32
    )
    sums_local = jnp.dot(mask_half[None, :], embeddings, preferred_element_type=jnp.float32)[0]
    count, sums = lax.psum((count_local, sums_local), ("wide", "narrow"))
    term = shifted_scatter(gram, count_local, sums_local, sums / count)
    level_rows = narrow_rows(term)
    own_rows = lax.psum(level_rows, "wide")
    center = sums / count
    cov_rows = own_rows / count
    ident_rows = (
        lax.broadcasted_iota(jnp.int32, (row_span, width), 0) + offset
        == lax.broadcasted_iota(jnp.int32, (row_span, width), 1)
    ).astype(jnp.float32)
    diag_block = lax.dynamic_slice_in_dim(cov_rows, offset, row_span, 1)
    trace_part = jnp.sum(jnp.diagonal(diag_block))
    square_part = jnp.sum(cov_rows * cov_rows)
    trace_cov, square_sum = lax.psum((trace_part, square_part), "narrow")
    ridge_add = 0.05 * trace_cov / width + 1e-06
    norm_frob = jnp.sqrt(square_sum + 2.0 * ridge_add * trace_cov + width * ridge_add * ridge_add)
    base_rows = (cov_rows + ridge_add * ident_rows) / norm_frob
    root_rows = (3.0 * ident_rows - base_rows) / 2.0
    root_full = lax.all_gather(root_rows, "narrow", axis=0, tiled=True)
    first = jnp.dot(
        base_rows, root_full, precision=lax.Precision.HIGHEST, preferred_element_type=jnp.float32
    )
    second = jnp.dot(
        first, root_full, precision=lax.Precision.HIGHEST, preferred_element_type=jnp.float32
    )
    factor = (3.0 * ident_rows - second) / 2.0
    root_rows = jnp.dot(
        factor, root_full, precision=lax.Precision.HIGHEST, preferred_element_type=jnp.float32
    )
    centered_x = embeddings.astype(jnp.float32) - center
    product = jnp.dot(
        centered_x,
        lax.all_gather(root_rows, "narrow", axis=0, tiled=True),
        precision=lax.Precision.HIGHEST,
        preferred_element_type=jnp.float32,
    )
    return (product / jnp.sqrt(norm_frob)).astype(jnp.bfloat16)


def solution(mesh):
    in_specs = (P(("wide", "narrow"), None), P(("wide", "narrow")))
    out_specs = P(("wide", "narrow"), None)
    return jax.shard_map(
        on_device, mesh=mesh, in_specs=in_specs, out_specs=out_specs, check_vma=False
    )
```

profile of v0, /device:TPU:0, one launch (start us, length us, event | category | flops | bytes accessed | tf_op | source)
XLA Modules:
  0.0 300.6 jit_solution(4755402428084836865)
XLA Ops:
  6.5 0.7 convert_element_type.14
  7.2 1.3 convert_reduce_fusion
  8.5 1.5 fusion.11
  10.0 42.1 %all-reduce = (f32[1024]{0:T(1024)S(1)}, f32[]{:T(128)}) all-reduce(f32[1024]{0:T(1024)S(1)} %bitcast.12, f32[]{:T(128)} %convert_reduce_fusion), channel_id=1, replica_groups=mesh['wide'=8,'narrow'=4] {'wide','narrow'}, use_global_device_ids=true, to_apply=%region_0.0 | all-reduce | flops 1025 | bytes 8200 | tf_op jit(solution)/shard_map/psum | solution.py:32
  52.1 1.3 broadcast_multiply_fusion
  53.4 5.3 %multiply_add_fusion = f32[1024,1024]{1,0:T(8,128)} fusion(bf16[512,1024]{1,0:T(8,128)(2,1)} %param.2, f32[1024]{0:T(1024)S(1)} %get-tuple-element.11, f32[1024]{0:T(1024)S(1)} %bitcast.13, f32[1024]{0:T(1024)S(1)} %get-tuple-element.12, bf16[512]{0:T(512)(128)(2,1)S(1)} %convert_element_type.14), kind=kOutput, calls=%fused_computation.1 | convolution fusion | flops 1080557568 | bytes 5256192 | tf_op jit(solution)/shard_map/dot_general | solution.py:28
  58.7 0.0 all-reduce.4.cloned.1.call-start
  58.8 44.7 %reduce-scatter.2.cloned.1.call-done = f32[256,1024]{1,0:T(8,128)} async-done(((f32[1024,1024]{1,0:T(8,128)}), f32[256,1024]{1,0:T(8,128)}) %reduce-scatter.2.cloned.1.call-update) | async-done | bytes 1048592 | tf_op jit(solution)/shard_map/reduce_scatter | solution.py:17
  103.5 0.0 all-reduce.4.cloned.1.call-update
  103.5 0.0 all-gather.3.cloned.1.call-start
  103.6 81.6 %all-reduce.4.cloned.1.call-done = f32[256,1024]{1,0:T(8,128)} async-done(((f32[256,1024]{1,0:T(8,128)}), f32[256,1024]{1,0:T(8,128)}) %all-reduce.4.cloned.1.call-update) | async-done | bytes 1048592 | tf_op jit(solution)/shard_map/psum | solution.py:35
  185.2 2.7 multiply_reduce_fusion
  188.0 2.3 gather_fusion
  190.4 0.7 reduce_sum.28
  191.0 7.2 %all-reduce.1 = (f32[]{:T(128)}, f32[]{:T(128)}) all-reduce(f32[]{:T(128)} %get-tuple-element.9, f32[]{:T(128)} %reduce_sum.28), channel_id=1, replica_groups=mesh['wide'=8,'narrow'=4] {'narrow'}, use_global_device_ids=true, to_apply=%region_8.9 | all-reduce | flops 2 | bytes 16 | tf_op jit(solution)/shard_map/psum | solution.py:45
  200.3 1.3 fusion.7
  201.6 0.0 all-gather.3.cloned.1.call-update
  201.6 0.2 all-gather.5.cloned.1.call-start
  201.8 33.4 %all-gather.3.cloned.1.call-done = f32[1024,1024]{1,0:T(8,128)} async-done(((f32[256,1024]{1,0:T(8,128)}), f32[1024,1024]{1,0:T(8,128)}) %all-gather.3.cloned.1.call-update) | async-done | bytes 4194320 | tf_op jit(solution)/shard_map/all_gather | solution.py:50
  235.2 6.1 %fusion.10 = f32[256,1024]{1,0:T(8,128)S(1)} fusion(f32[1024,1024]{1,0:T(8,128)} %all-gather.3.cloned.1.call-done, f32[256,1024]{1,0:T(8,128)S(1)} %get-tuple-element.10, f32[]{:T(128)S(6)} %sqrt.6, f32[]{:T(128)S(6)} %add.45, s32[256]{0:T(256)S(1)} %iota_add_fusion), kind=kOutput, calls=%fused_computation.23 | convolution fusion | flops 3222274048 | bytes 6292488 | tf_op jit(solution)/shard_map/dot_general | solution.py:51
  241.4 3.7 %fusion.4 = f32[256,1024]{1,0:T(8,128)S(1)} fusion(f32[256,1024]{1,0:T(8,128)S(1)} %fusion.10, f32[1024,1024]{1,0:T(8,128)S(1)} %copy-done, s32[256]{0:T(256)S(1)} %iota_add_fusion), kind=kOutput, calls=%fused_computation.9 | convolution fusion | flops 3222274048 | bytes 6292480 | tf_op jit(solution)/shard_map/dot_general | solution.py:54
  245.2 4.7 %fusion.12 = f32[256,1024]{1,0:T(8,128)} fusion(f32[256,1024]{1,0:T(8,128)S(1)} %fusion.4, f32[1024,1024]{1,0:T(8,128)S(1)} %copy-done), kind=kOutput, calls=%fused_computation.25 | convolution fusion | flops 3221225472 | bytes 6291456 | tf_op jit(solution)/shard_map/dot_general | solution.py:58
  249.9 34.6 %all-gather.5.cloned.1.call-done = f32[1024,1024]{1,0:T(8,128)} async-done(((f32[256,1024]{1,0:T(8,128)}), f32[1024,1024]{1,0:T(8,128)}) %all-gather.5.cloned.1.call-update) | async-done | bytes 4194320 | tf_op jit(solution)/shard_map/all_gather | solution.py:64
  284.5 9.6 %divide_convert_fusion = bf16[512,1024]{1,0:T(8,128)(2,1)} fusion(f32[1024,1024]{1,0:T(8,128)} %all-gather.5.cloned.1.call-done, bf16[512,1024]{1,0:T(8,128)(2,1)S(1)} %copy-done.1, f32[]{:T(128)S(6)} %sqrt.7, f32[1024]{0:T(1024)S(1)} %get-tuple-element.12), kind=kOutput, calls=%fused_computation.2 | convolution fusion | flops 6444548096 | bytes 6295556 | tf_op jit(solution)/shard_map/dot_general | solution.py:62
  (11 shorter events, 0.1 us)
Async XLA Ops:
  6.5 97.0 %reduce-scatter.2.cloned.1.call-start = ((), (), s32[]{:S(2)}) async-start(), calls=%async_computation.1 | async-start | bytes 5242880 | tf_op jit(solution)/shard_map/reduce_scatter | solution.py:17
  58.7 126.5 %all-reduce.4.cloned.1.call-start = ((), (), s32[]{:S(2)}) async-start(), calls=%async_computation.2 | async-start | bytes 2097152 | tf_op jit(solution)/shard_map/psum | solution.py:35
  103.5 131.7 %all-gather.3.cloned.1.call-start = ((), (), s32[]{:S(2)}) async-start(), calls=%async_computation.3 | async-start | bytes 5242880 | tf_op jit(solution)/shard_map/all_gather | solution.py:50
  201.6 82.9 %all-gather.5.cloned.1.call-start = ((), (), s32[]{:S(2)}) async-start(), calls=%async_computation.4 | async-start | bytes 5242880 | tf_op jit(solution)/shard_map/all_gather | solution.py:64
  235.2 6.1 %copy-start = (f32[1024,1024]{1,0:T(8,128)S(1)}, f32[1024,1024]{1,0:T(8,128)}, u32[]{:S(2)}) copy-start(f32[1024,1024]{1,0:T(8,128)} %all-gather.3.cloned.1.call-done) | copy-start | bytes 12582916
  245.1 39.3 %copy-start.1 = (bf16[512,1024]{1,0:T(8,128)(2,1)S(1)}, bf16[512,1024]{1,0:T(8,128)(2,1)}, u32[]{:S(2)}) copy-start(bf16[512,1024]{1,0:T(8,128)(2,1)} %param.2) | copy-start | bytes 3145732
Sparse Core Ops, SparseCore 0:
  58.9 44.6 reduce-scatter.1
  107.0 78.1 all-reduce.3
  201.7 33.4 all-gather.2
  250.0 34.4 all-gather.4
where the time goes:
time: 301 us
  waiting for transfers between devices  194 us (64%)
  blocking collectives  49.3 us (16%)
  matrix products  30.9 us (10%)
  between operations  15.3 us (5%)
  other arithmetic  7.97 us (3%)
    psum x1, waiting for transfers between devices, on_device(): own_rows = lax.psum(level_rows, 'wide')  81.6 us
    reduce_scatter x1, waiting for transfers between devices, narrow_rows(): return lax.psum_scatter(term, 'narrow', scatter_dimension=0, tiled=True)  44.7 us
    psum x1, blocking collectives, on_device(): count, sums = lax.psum((count_local, sums_local), ('wide', 'narrow'))  42.1 us
    all_gather x1, waiting for transfers between devices, on_device(): lax.all_gather(root_rows, 'narrow', axis=0, tiled=True)  34.6 us
    all_gather x1, waiting for transfers between devices, on_device(): root_full = lax.all_gather(root_rows, 'narrow', axis=0, tiled=True)  33.4 us
    dot_general x1, matrix products, on_device(): jnp.dot(centered_x, lax.all_gather(root_rows, 'narrow', axis=0, tiled=Tru...  9.62 us
    psum x1, blocking collectives, on_device(): trace_cov, square_sum = lax.psum((trace_part, square_part), 'narrow')  7.19 us
    dot_general x1, matrix products, on_device(): jnp.dot(base_rows, root_full, precision=lax.Precision.HIGHEST, preferred_...  6.13 us
  transfers between devices with their start and end apart: 4, of which 4 were waited for; matrix products, arithmetic and copies ran while one was open for 0% of the time, Pallas kernels for 0%

commit v1 on v0

--- a/solution.py
+++ b/solution.py
@@ -29,7 +29,7 @@
         masked, embeddings, (((0,), (0,)), ((), ())), preferred_element_type=jnp.float32
     )
     sums_local = jnp.dot(mask_half[None, :], embeddings, preferred_element_type=jnp.float32)[0]
-    count, sums = lax.psum((count_local, sums_local), ("wide", "narrow"))
+    count, sums = lax.psum(lax.psum((count_local, sums_local), "wide"), "narrow")
     term = shifted_scatter(gram, count_local, sums_local, sums / count)
     level_rows = narrow_rows(term)
     own_rows = lax.psum(level_rows, "wide")

time: 301 us -> 287 us (0.953)
  blocking collectives: 49.3 us -> 37.7 us
    psum x1 -> x2, blocking collectives: 42.1 us -> 30.5 us  [the longest x1 24.1 us: on_device(): lax.psum((count_local, sums_local), 'wide')]
where the time goes in v1:
time: 287 us; the launch traced here: 286 us
  waiting for transfers between devices  192 us (67%)
  blocking collectives  37.7 us (13%)
  matrix products  31 us (11%)
  between operations  15.3 us (5%)
  other arithmetic  7.97 us (3%)
    psum x1, waiting for transfers between devices, on_device(): own_rows = lax.psum(level_rows, 'wide')  81.6 us
    reduce_scatter x1, waiting for transfers between devices, narrow_rows(): return lax.psum_scatter(term, 'narrow', scatter_dimension=0, tiled=True)  42.2 us
    all_gather x1, waiting for transfers between devices, on_device(): lax.all_gather(root_rows, 'narrow', axis=0, tiled=True)  34.6 us
    all_gather x1, waiting for transfers between devices, on_device(): root_full = lax.all_gather(root_rows, 'narrow', axis=0, tiled=True)  33.4 us
    psum x1, blocking collectives, on_device(): lax.psum((count_local, sums_local), 'wide')  24.1 us
    dot_general x1, matrix products, on_device(): jnp.dot(centered_x, lax.all_gather(root_rows, 'narrow', axis=0, tiled=Tru...  9.62 us
    psum x1, blocking collectives, on_device(): trace_cov, square_sum = lax.psum((trace_part, square_part), 'narrow')  7.19 us
    psum x1, blocking collectives, on_device(): lax.psum(lax.psum((count_local, sums_local), 'wide'), 'narrow')  6.4 us
  transfers between devices with their start and end apart: 4, of which 4 were waited for; matrix products, arithmetic and copies ran while one was open for 0% of the time, Pallas kernels for 0%

profile of v1, /device:TPU:0, one launch (start us, length us, event | category | flops | bytes accessed | tf_op | source)
XLA Modules:
  0.0 286.4 jit_solution(6015564478471303551)
XLA Ops:
  6.5 0.7 convert_element_type.14
  7.2 1.3 convert_reduce_fusion
  8.5 1.5 fusion.11
  10.0 24.1 %all-reduce = (f32[1024]{0:T(1024)S(1)}, f32[]{:T(128)}) all-reduce(f32[1024]{0:T(1024)S(1)} %bitcast.12, f32[]{:T(128)} %convert_reduce_fusion), channel_id=1, replica_groups=mesh['wide'=8,'narrow'=4] {'wide'}, use_global_device_ids=true, to_apply=%region_0.0 | all-reduce | flops 1025 | bytes 8200 | tf_op jit(solution)/shard_map/psum | solution.py:32
  34.1 6.4 %all-reduce.2 = (f32[1024]{0:T(1024)S(1)}, f32[]{:T(128)}) all-reduce(f32[1024]{0:T(1024)S(1)} %get-tuple-element.5, f32[]{:T(128)} %get-tuple-element.6), channel_id=1, replica_groups=mesh['wide'=8,'narrow'=4] {'narrow'}, use_global_device_ids=true, to_apply=%region_1.0 | all-reduce | flops 1025 | bytes 8200 | tf_op jit(solution)/shard_map/psum | solution.py:32
  40.4 1.3 broadcast_multiply_fusion
  41.7 5.3 %multiply_add_fusion = f32[1024,1024]{1,0:T(8,128)} fusion(bf16[512,1024]{1,0:T(8,128)(2,1)} %param.2, f32[1024]{0:T(1024)S(1)} %get-tuple-element.13, f32[1024]{0:T(1024)S(1)} %bitcast.13, f32[1024]{0:T(1024)S(1)} %get-tuple-element.14, bf16[512]{0:T(512)(128)(2,1)S(1)} %convert_element_type.14), kind=kOutput, calls=%fused_computation.1 | convolution fusion | flops 1080557568 | bytes 5256192 | tf_op jit(solution)/shard_map/dot_general | solution.py:28
  47.1 0.0 all-reduce.5.cloned.1.call-start
  47.1 42.2 %reduce-scatter.2.cloned.1.call-done = f32[256,1024]{1,0:T(8,128)} async-done(((f32[1024,1024]{1,0:T(8,128)}), f32[256,1024]{1,0:T(8,128)}) %reduce-scatter.2.cloned.1.call-update) | async-done | bytes 1048592 | tf_op jit(solution)/shard_map/reduce_scatter | solution.py:17
  89.3 0.0 all-reduce.5.cloned.1.call-update
  89.3 0.0 all-gather.3.cloned.1.call-start
  89.4 81.6 %all-reduce.5.cloned.1.call-done = f32[256,1024]{1,0:T(8,128)} async-done(((f32[256,1024]{1,0:T(8,128)}), f32[256,1024]{1,0:T(8,128)}) %all-reduce.5.cloned.1.call-update) | async-done | bytes 1048592 | tf_op jit(solution)/shard_map/psum | solution.py:35
  171.0 2.7 multiply_reduce_fusion
  173.8 2.3 gather_fusion
  176.1 0.7 reduce_sum.28
  176.8 7.2 %all-reduce.1 = (f32[]{:T(128)}, f32[]{:T(128)}) all-reduce(f32[]{:T(128)} %get-tuple-element.11, f32[]{:T(128)} %reduce_sum.28), channel_id=1, replica_groups=mesh['wide'=8,'narrow'=4] {'narrow'}, use_global_device_ids=true, to_apply=%region_10.11 | all-reduce | flops 2 | bytes 16 | tf_op jit(solution)/shard_map/psum | solution.py:45
  186.1 1.3 fusion.7
  187.4 0.2 all-gather.5.cloned.1.call-start
  187.6 33.4 %all-gather.3.cloned.1.call-done = f32[1024,1024]{1,0:T(8,128)} async-done(((f32[256,1024]{1,0:T(8,128)}), f32[1024,1024]{1,0:T(8,128)}) %all-gather.3.cloned.1.call-update) | async-done | bytes 4194320 | tf_op jit(solution)/shard_map/all_gather | solution.py:50
  221.0 6.1 %fusion.10 = f32[256,1024]{1,0:T(8,128)S(1)} fusion(f32[1024,1024]{1,0:T(8,128)} %all-gather.3.cloned.1.call-done, f32[256,1024]{1,0:T(8,128)S(1)} %get-tuple-element.12, f32[]{:T(128)S(6)} %sqrt.6, f32[]{:T(128)S(6)} %add.49, s32[256]{0:T(256)S(1)} %iota_add_fusion), kind=kOutput, calls=%fused_computation.23 | convolution fusion | flops 3222274048 | bytes 6292488 | tf_op jit(solution)/shard_map/dot_general | solution.py:51
  227.2 3.7 %fusion.4 = f32[256,1024]{1,0:T(8,128)S(1)} fusion(f32[256,1024]{1,0:T(8,128)S(1)} %fusion.10, f32[1024,1024]{1,0:T(8,128)S(1)} %copy-done, s32[256]{0:T(256)S(1)} %iota_add_fusion), kind=kOutput, calls=%fused_computation.9 | convolution fusion | flops 3222274048 | bytes 6292480 | tf_op jit(solution)/shard_map/dot_general | solution.py:54
  230.9 4.7 %fusion.12 = f32[256,1024]{1,0:T(8,128)} fusion(f32[256,1024]{1,0:T(8,128)S(1)} %fusion.4, f32[1024,1024]{1,0:T(8,128)S(1)} %copy-done), kind=kOutput, calls=%fused_computation.25 | convolution fusion | flops 3221225472 | bytes 6291456 | tf_op jit(solution)/shard_map/dot_general | solution.py:58
  235.7 34.6 %all-gather.5.cloned.1.call-done = f32[1024,1024]{1,0:T(8,128)} async-done(((f32[256,1024]{1,0:T(8,128)}), f32[1024,1024]{1,0:T(8,128)}) %all-gather.5.cloned.1.call-update) | async-done | bytes 4194320 | tf_op jit(solution)/shard_map/all_gather | solution.py:64
  270.2 9.6 %divide_convert_fusion = bf16[512,1024]{1,0:T(8,128)(2,1)} fusion(f32[1024,1024]{1,0:T(8,128)} %all-gather.5.cloned.1.call-done, bf16[512,1024]{1,0:T(8,128)(2,1)S(1)} %copy-done.1, f32[]{:T(128)S(6)} %sqrt.7, f32[1024]{0:T(1024)S(1)} %get-tuple-element.14), kind=kOutput, calls=%fused_computation.2 | convolution fusion | flops 6444548096 | bytes 6295556 | tf_op jit(solution)/shard_map/dot_general | solution.py:62
  (12 shorter events, 0.1 us)
Async XLA Ops:
  6.5 82.8 %reduce-scatter.2.cloned.1.call-start = ((), (), s32[]{:S(2)}) async-start(), calls=%async_computation.1 | async-start | bytes 5242880 | tf_op jit(solution)/shard_map/reduce_scatter | solution.py:17
  47.1 123.9 %all-reduce.5.cloned.1.call-start = ((), (), s32[]{:S(2)}) async-start(), calls=%async_computation.2 | async-start | bytes 2097152 | tf_op jit(solution)/shard_map/psum | solution.py:35
  89.3 131.7 %all-gather.3.cloned.1.call-start = ((), (), s32[]{:S(2)}) async-start(), calls=%async_computation.3 | async-start | bytes 5242880 | tf_op jit(solution)/shard_map/all_gather | solution.py:50
  187.4 82.9 %all-gather.5.cloned.1.call-start = ((), (), s32[]{:S(2)}) async-start(), calls=%async_computation.4 | async-start | bytes 5242880 | tf_op jit(solution)/shard_map/all_gather | solution.py:64
  221.0 6.1 %copy-start = (f32[1024,1024]{1,0:T(8,128)S(1)}, f32[1024,1024]{1,0:T(8,128)}, u32[]{:S(2)}) copy-start(f32[1024,1024]{1,0:T(8,128)} %all-gather.3.cloned.1.call-done) | copy-start | bytes 12582916
  230.9 39.3 %copy-start.1 = (bf16[512,1024]{1,0:T(8,128)(2,1)S(1)}, bf16[512,1024]{1,0:T(8,128)(2,1)}, u32[]{:S(2)}) copy-start(bf16[512,1024]{1,0:T(8,128)(2,1)} %param.2) | copy-start | bytes 3145732
Sparse Core Ops, SparseCore 0:
  47.2 42.0 reduce-scatter.1
  92.8 78.1 all-reduce.4
  187.5 33.4 all-gather.2
  235.7 34.4 all-gather.4
